TPU v7x, 128 devices: a whole 4x4x4 slice. The times are simulated.
128 devices in a mesh: split: 16 (over x, y_hi, core), shard: 8 (over y_lo, z).
Axes of the slice: x: 4, y: 4 (y_hi: 2, y_lo: 2; y = y_hi * 2 + y_lo), z: 4, core: 2. Of those that a mesh axis runs over, the one named last changes fastest.
Arguments:
- strain: bfloat16 [3, 4096], P(None, ('split', 'shard')), may hold values from -6 to 6
- basis: bfloat16 [16, 400, 2048], P('split', 'shard'), may hold values from -0.125 to 0.125
- recon: bfloat16 [16, 2, 4096, 400], P('split', None, 'shard'), may hold values from -0.3125 to 0.3125
Outputs:
- snr2: float32 [16, 4096, 2048], P('split', 'shard')
- loudest: float32 [2048], replicated
All inputs are finite; a program needn't handle non-finite values.
Results may differ from a plain program's by a relative error of at most 0.0025.
Values may be sent and summed in bfloat16 or wider, within the bound.
No kernel may reach another device: no remote copies, remote signals or barrier semaphores. Data moves between devices by JAX's collectives and lax.ppermute only.
A program may use at most 128 MiB of HBM per device.

v0:
```python
import jax
import jax.numpy as jnp
from jax import lax
from jax.sharding import PartitionSpec as P


def toeplitz_block(segment, rows, cols):
    width = rows + cols - 1
    turned = jnp.concatenate([segment[rows - 1 :], segment[: rows - 1]])
    flat = jnp.broadcast_to(turned, (rows, width)).reshape(-1)[: rows * (width - 1)]
    return flat.reshape(rows, width - 1)[:, :cols]


def filter_series(signal, filters):
    taps = filters.shape[1]
    tout = signal.shape[0] - taps
    tblock = min(512, tout)
    kblock = min(512, taps)
    outputs = []
    for tpos in range(tout // tblock):
        pieces = []
        for kpos in range(taps // kblock):
            begin = tpos * tblock + taps - (kpos + 1) * kblock
            segment = signal[begin : begin + kblock + tblock - 1]
            pieces.append(toeplitz_block(segment, kblock, tblock))
        frame = jnp.concatenate(pieces, axis=0)
        outputs.append(jnp.dot(filters, frame, preferred_element_type=jnp.float32))
    return jnp.concatenate(outputs, axis=1)


def all_detectors(whole, filters):
    return jnp.stack(
        [filter_series(whole[det], filters).astype(jnp.bfloat16) for det in range(whole.shape[0])]
    )


def per_device(strain, basis, recon):
    whole = lax.all_gather(strain, ("split", "shard"), axis=1, tiled=True)
    filters = basis[0]
    own_series = all_detectors(whole, filters)
    series = lax.all_gather(own_series, "shard", axis=1, tiled=True)
    weights = recon[0]
    detectors = series.shape[0]
    scale = 1.0 / (2.0 * detectors)
    templ = weights.shape[1]
    mblock = min(256, templ)
    blocks = []
    for mpos in range(templ // mblock):
        part = weights[:, mpos * mblock : (mpos + 1) * mblock]
        total = jnp.zeros((mblock, series.shape[2]), jnp.float32)
        for det in range(detectors):
            zvals = jnp.einsum("qml,lt->qmt", part, series[det], preferred_element_type=jnp.float32)
            total = total + jnp.sum(zvals * zvals, axis=0)
        blocks.append(total * scale)
    snr_local = jnp.concatenate(blocks, axis=0)
    loudest = lax.pmax(jnp.max(snr_local, axis=0), ("split", "shard"))
    return (snr_local[None], loudest)


def solution(mesh):
    return jax.shard_map(
        per_device,
        mesh=mesh,
        in_specs=(
            P(None, ("split", "shard")),
            P("split", "shard", None),
            P("split", None, "shard", None),
        ),
        out_specs=(P("split", "shard", None), P()),
        check_vma=False,
    )
```

profile of v0, /device:TPU:1, one launch (start us, length us, event | category | flops | bytes accessed | tf_op | source)
XLA Modules:
  0.0 618.8 jit_solution(15885630971313744312)
XLA Ops:
  7.2 303.4 %all-gather = bf16[128,32,3]{1,2,0:T(4,128)(2,1)S(1)} all-gather(bf16[1,32,3]{1,2,0:T(4,128)(2,1)} %bitcast.105), channel_id=1, replica_groups=mesh['split'=16,'shard'=8] {'split','shard'}, dimensions={0}, use_global_device_ids=true | all-gather | bytes 24768 | tf_op jit(solution)/shard_map/all_gather | solution.py:38
  315.4 1.8 reshape.429
  319.9 1.8 reshape.433
  324.5 1.8 reshape.435
  327.3 2.0 reshape.436
  329.4 1.8 reshape.437
  333.1 1.8 reshape.439
  345.0 1.8 reshape.444
  346.9 1.8 reshape.445
  352.6 1.9 fusion.144
  356.9 1.8 reshape.449
  360.7 1.9 reshape.450
  362.6 1.8 reshape.451
  364.5 2.2 fusion.153
  368.6 1.8 reshape.453
  373.2 1.8 reshape.455
  388.5 2.5 fusion.156
  395.9 2.3 fusion.162
  398.3 1.8 reshape.464
  402.2 2.1 fusion.165
  423.7 84.6 %all-gather.3.cloned.1.call-done = bf16[3,400,2048]{2,0,1:T(4,128)(2,1)} async-done(((bf16[3,50,2048]{2,0,1:T(4,128)(2,1)}), bf16[3,400,2048]{2,0,1:T(4,128)(2,1)}) %all-gather.3.cloned.1.call-update) | async-done | bytes 4915216 | tf_op jit(solution)/shard_map/all_gather | solution.py:41
  508.3 15.7 %fusion.202 = (bf16[1,400,2048]{2,0,1:T(2,128)(2,1)S(1)}, bf16[1,400,2048]{2,0,1:T(2,128)(2,1)S(1)}, bf16[1,400,2048]{2,0,1:T(2,128)(2,1)S(1)}) fusion(bf16[3,400,2048]{2,0,1:T(4,128)(2,1)} %all-gather.3.cloned.1.call-done), kind=kLoop, calls=%fused_computation.230 | loop fusion | bytes 9830400 | tf_op jit(solution)/shard_map/slice | solution.py:52
  524.0 2.0 multiply_reduce_fusion.1
  526.0 2.0 multiply_reduce_fusion.4
  528.0 2.0 multiply_reduce_fusion.2
  530.0 2.0 multiply_reduce_fusion.5
  532.0 2.0 multiply_reduce_fusion
  534.0 2.0 multiply_reduce_fusion.3
  536.0 1.9 fusion.198
  537.9 64.2 %pmax.7 = f32[2048]{0:T(1024)} all-reduce(f32[2048]{0:T(1024)S(1)} %reduce_max.19), channel_id=1, replica_groups=mesh['split'=16,'shard'=8] {'split','shard'}, use_global_device_ids=true, to_apply=%region_8.9 | all-reduce | flops 2048 | bytes 16384 | tf_op jit(solution)/shard_map/pmax | solution.py:56
  602.1 4.1 maximum_bitcast_fusion
  606.2 5.3 copy.11
  (228 shorter events, 75.1 us)
Async XLA Ops:
  7.2 345.4 %copy-start = (bf16[1,50,2048]{2,1,0:T(8,128)(2,1)S(1)}, bf16[1,50,2048]{2,1,0:T(8,128)(2,1)}, u32[]{:S(2)}) copy-start(bf16[1,50,2048]{2,1,0:T(8,128)(2,1)} %param.4) | copy-start | bytes 614404
  7.2 501.1 %all-gather.3.cloned.1.call-start = ((), (), s32[]{:S(2)}) async-start(), calls=%async_computation | async-start | bytes 7372800 | tf_op jit(solution)/shard_map/all_gather | solution.py:41
  350.7 1.9 slice-start.1
  350.7 1.9 copy-start.8
  352.6 1.9 copy-start.12
  352.6 1.9 copy-start.10
  352.6 1.9 copy-start.16
  362.5 2.0 copy-start.13
  364.5 2.2 copy-start.37
  364.5 2.2 copy-start.40
  368.5 2.8 copy-start.35
  368.5 2.8 copy-start.38
  373.1 2.8 copy-start.33
  373.1 2.7 copy-start.36
  377.6 2.8 copy-start.31
  377.7 2.8 copy-start.34
  386.5 1.9 slice-start.2
  386.5 1.9 copy-start.9
  388.4 2.5 copy-start.14
  388.5 2.5 copy-start.11
  388.5 2.5 copy-start.17
  395.8 2.3 copy-start.20
  395.9 2.3 copy-start.28
  400.2 2.0 copy-start.15
  402.1 2.2 copy-start.26
  406.1 1.9 copy-start.44
  406.1 1.9 copy-start.45
  410.8 2.8 copy-start.42
  410.8 2.8 copy-start.43
  415.4 2.0 slice-start
  415.4 2.0 copy-start.6
  423.7 100.3 %copy-start.46 = (bf16[1,2,512,400]{2,3,1,0:T(8,128)(2,1)S(1)}, bf16[1,2,512,400]{2,3,1,0:T(8,128)(2,1)}, u32[]{:S(2)}) copy-start(bf16[1,2,512,400]{2,3,1,0:T(8,128)(2,1)} %param.5) | copy-start | bytes 2457604
  (20 other events, 27.6 us)
Sparse Core Ops, SparseCore 0:
  423.8 84.4 all-gather.2
where the time goes:
time: 628 us; the launch traced here: 619 us
  blocking collectives  368 us (59%)
  local copies, waits for them, and re-layouts  115 us (18%)
  waiting for transfers between devices  84.6 us (13%)
  matrix products  29.4 us (5%)
  between operations  15.9 us (3%)
  other arithmetic  6.67 us (1%)
    all_gather x1, blocking collectives, per_device(): whole = lax.all_gather(strain, ('split', 'shard'), axis=1, tiled=True)  303 us
    all_gather x1, waiting for transfers between devices, per_device(): series = lax.all_gather(own_series, 'shard', axis=1, tiled=True)  84.6 us
    pmax x1, blocking collectives, per_device(): loudest = lax.pmax(jnp.max(snr_local, axis=0), ('split', 'shard'))  64.2 us
    reshape x21, local copies, waits for them, and re-layouts, toeplitz_block(): return flat.reshape(rows, width - 1)[:, :cols]  38.2 us
    reshape x21, local copies, waits for them, and re-layouts, toeplitz_block(): jnp.broadcast_to(turned, (rows, width)).reshape(-1)[:rows * (width - 1)]  35.8 us
    dot_general x12, matrix products, filter_series(): outputs.append(jnp.dot(filters, frame, preferred_element_type=jnp.float32))  17.4 us
    slice x1, local copies, waits for them, and re-layouts, per_device(): series[det]  15.7 us
  transfers between devices with their start and end apart: 1, of which 1 were waited for; matrix products, arithmetic and copies ran while one was open for 0% of the time, Pallas kernels for 0%

commit v1 on v0

--- a/solution.py
+++ b/solution.py
@@ -38,7 +38,10 @@
     whole = lax.all_gather(strain, ("split", "shard"), axis=1, tiled=True)
     filters = basis[0]
     own_series = all_detectors(whole, filters)
-    series = lax.all_gather(own_series, "shard", axis=1, tiled=True)
+    block_out = tuple((own_series for _ in range(lax.axis_size("shard"))))
+    b_now = jnp.stack(block_out, 0)
+    base_arr = lax.all_to_all(b_now, "shard", 0, 0)
+    series = jnp.concatenate(base_arr, axis=1)
     weights = recon[0]
     detectors = series.shape[0]
     scale = 1.0 / (2.0 * detectors)

time: 628 us -> 595 us (0.947)
  waiting for transfers between devices: 84.6 us -> 0 us
  blocking collectives: 368 us -> 432 us
  between operations: 15.9 us -> 2.46 us
    all_gather x1 -> x0, waiting for transfers between devices: 84.6 us -> none  [per_device(): series = lax.all_gather(own_series, 'shard', axis=1, tiled=True)]
    all_to_all x0 -> x1, blocking collectives: none -> 48.5 us  [per_device(): base_arr = lax.all_to_all(b_now, 'shard', 0, 0)]
    pmax x1, blocking collectives: 64.2 us -> 80.1 us  [per_device(): loudest = lax.pmax(jnp.max(snr_local, axis=0), ('split', 'shard'))]
    slice x1, local copies, waits for them, and re-layouts: 15.7 us -> 2.46 us  [per_device(): series[det]]
    squeeze x0 -> x3, local copies, waits for them, and re-layouts: none -> 6.63 us  [per_device(): series[det]]
  transfers between devices with their start and end apart: 1 -> 0, of which waited for: 1 -> 0; matrix products, arithmetic and copies ran while one was open for 0% -> 0% of each run, Pallas kernels for 0% -> 0%
where the time goes in v1:
time: 595 us; the launch traced here: 586 us
  blocking collectives  432 us (73%)
  local copies, waits for them, and re-layouts  110 us (18%)
  matrix products  35.5 us (6%)
  other arithmetic  6.61 us (1%)
    all_gather x1, blocking collectives, per_device(): whole = lax.all_gather(strain, ('split', 'shard'), axis=1, tiled=True)  303 us
    pmax x1, blocking collectives, per_device(): loudest = lax.pmax(jnp.max(snr_local, axis=0), ('split', 'shard'))  80.1 us
    all_to_all x1, blocking collectives, per_device(): base_arr = lax.all_to_all(b_now, 'shard', 0, 0)  48.5 us
    reshape x21, local copies, waits for them, and re-layouts, toeplitz_block(): return flat.reshape(rows, width - 1)[:, :cols]  38.4 us
    reshape x21, local copies, waits for them, and re-layouts, toeplitz_block(): jnp.broadcast_to(turned, (rows, width)).reshape(-1)[:rows * (width - 1)]  35.8 us
    dot_general x6, matrix products, per_device(): jnp.einsum('qml,lt->qmt', part, series[det], preferred_element_type=jnp.f...  18.1 us
    dot_general x12, matrix products, filter_series(): outputs.append(jnp.dot(filters, frame, preferred_element_type=jnp.float32))  17.4 us

profile of v1, /device:TPU:1, one launch (start us, length us, event | category | flops | bytes accessed | tf_op | source)
XLA Modules:
  0.0 586.2 jit_solution(10999948318656270127)
XLA Ops:
  0.6 303.4 %all-gather = bf16[128,32,3]{1,2,0:T(4,128)(2,1)S(1)} all-gather(bf16[1,32,3]{1,2,0:T(4,128)(2,1)} %bitcast.104), channel_id=1, replica_groups=mesh['split'=16,'shard'=8] {'split','shard'}, dimensions={0}, use_global_device_ids=true | all-gather | bytes 24768 | tf_op jit(solution)/shard_map/all_gather | solution.py:38
  308.8 1.8 reshape.441
  313.4 1.8 reshape.445
  317.9 1.8 reshape.447
  320.7 2.0 reshape.448
  322.8 1.8 reshape.449
  326.5 1.8 reshape.451
  338.4 1.8 reshape.456
  340.3 1.8 reshape.457
  346.0 1.9 fusion.144
  354.1 1.9 reshape.462
  356.1 1.8 reshape.463
  358.0 2.2 fusion.153
  362.0 1.8 reshape.465
  381.8 2.5 fusion.156
  389.2 2.3 fusion.162
  391.7 1.8 reshape.476
  395.5 2.1 fusion.165
  408.8 2.0 reshape.439
  416.6 48.5 %all_to_all.5 = bf16[8,3,50,2048]{3,2,1,0:T(8,128)(2,1)S(1)} all-to-all(bf16[8,3,50,2048]{3,2,1,0:T(8,128)(2,1)S(1)} %stack.5), channel_id=1, replica_groups=mesh['split'=16,'shard'=8] {'shard'}, dimensions={0} | all-to-all | bytes 9830400 | tf_op jit(solution)/shard_map/all_to_all | solution.py:43
  465.0 2.5 fusion.202
  467.5 2.7 reshape.481
  470.2 4.3 multiply_reduce_fusion.2
  474.5 2.6 multiply_reduce_fusion.5
  477.1 2.6 reshape.483
  479.7 4.3 multiply_reduce_fusion
  483.9 2.6 multiply_reduce_fusion.3
  488.0 3.0 multiply_reduce_fusion.1
  494.4 1.9 fusion.198
  496.3 80.1 %pmax.7 = f32[2048]{0:T(1024)} all-reduce(f32[2048]{0:T(1024)S(1)} %reduce_max.19), channel_id=1, replica_groups=mesh['split'=16,'shard'=8] {'split','shard'}, use_global_device_ids=true, to_apply=%region_8.9 | all-reduce | flops 2048 | bytes 16384 | tf_op jit(solution)/shard_map/pmax | solution.py:59
  576.4 4.1 maximum_bitcast_fusion
  580.5 5.3 copy.7
  (243 shorter events, 80.9 us)
Async XLA Ops:
  0.6 345.3 %copy-start = (bf16[1,50,2048]{2,1,0:T(8,128)(2,1)S(1)}, bf16[1,50,2048]{2,1,0:T(8,128)(2,1)}, u32[]{:S(2)}) copy-start(bf16[1,50,2048]{2,1,0:T(8,128)(2,1)} %param.4) | copy-start | bytes 614404
  346.0 1.9 copy-start.19
  346.0 1.9 copy-start.17
  356.0 2.0 copy-start.20
  357.9 2.2 copy-start.44
  357.9 2.2 copy-start.47
  361.9 2.8 copy-start.42
  361.9 2.8 copy-start.45
  366.5 2.8 copy-start.40
  366.5 2.7 copy-start.43
  371.1 2.8 copy-start.38
  371.1 2.8 copy-start.41
  381.8 2.5 copy-start.21
  381.8 2.5 copy-start.18
  381.8 2.5 copy-start.24
  389.2 2.3 copy-start.27
  389.2 2.3 copy-start.35
  393.5 2.0 copy-start.22
  395.5 2.2 copy-start.33
  399.5 1.9 copy-start.51
  399.5 1.9 copy-start.52
  404.1 2.8 copy-start.49
  404.1 2.8 copy-start.50
  408.7 2.2 slice-start
  408.7 2.2 copy-start.13
  467.5 2.7 copy-start.53
  470.2 4.3 copy-start.9
  479.7 4.3 copy-start.10
  488.0 3.0 copy-start.11
  491.0 2.2 copy-start.6
  491.0 2.8 copy-start.7
  491.0 3.4 copy-start.8
  (26 other events, 38.7 us)
